TPU v7x, 512 devices: a whole 4x4x16 slice. The times are simulated.
512 devices in a mesh: gx: 32 (over x, y, core), gy: 16 (over z).
Axes of the slice: x: 4, y: 4, z: 16, core: 2. Of those that a mesh axis runs over, the one named last changes fastest.
Arguments:
- right_side: float32 [4096, 2048], P('gx', 'gy'), may hold values from -6 to 6
- shift: float32 [4096, 2048], P('gx', 'gy'), may hold values from 0.02 to 0.5
- face_x: float32 [4096, 2048], P('gx', 'gy'), may hold values from 0.3 to 5
- face_y: float32 [4096, 2048], P('gx', 'gy'), may hold values from 0.3 to 5
- ice_mask: int32 [4096, 2048], P('gx', 'gy'), may hold values 0 or 1
- deflation: float32 [32, 4096, 2048], P(None, 'gx', 'gy'), may hold values from -6 to 6
- coarse_matrix: float32 [16, 1024, 1024], P('gy', 'gx'), as said below
Outputs:
- solution_field: float32 [4096, 2048], P('gx', 'gy')
- residual: float32 [4096, 2048], P('gx', 'gy')
Inputs may be any that keep to these rules, and one draw needn't show every extreme that they name: Each coarse_matrix[b] is symmetric positive definite.
All inputs are finite; a program needn't handle non-finite values. No bound on the sum of `ice_mask` on one device may be relied on, other than what follows from the above.
Results may differ from a plain program's by a relative error of at most 0.0023.
Values sent between devices are 32-bit elements; how exact they have to be, the bound alone decides.
A program may use at most 64 MiB of HBM per device.

v0:
```python
import functools

import jax
import jax.numpy as jnp
from jax import lax
from jax.experimental import pallas as pl
from jax.experimental.pallas import tpu as pltpu
from jax.sharding import PartitionSpec as P

HIGH = lax.Precision.HIGHEST
MESH = pl.DeviceIdType.MESH
VMEM = pltpu.VMEM
SIDE = 4
B = 128
W = 8
TILES = B // W
GROUP = 4


def along_gx(index):
    return {"gx": index}


def gather_kernel(own_ref, whole, local_sem, send_sem, near_sem, far_sem, core_sem, core_send):
    rows = own_ref.shape[0]
    half = rows // 2
    me = lax.axis_index("gx")
    core = lax.rem(me, 2)
    y = lax.rem(me // 2, SIDE)
    x = me // (2 * SIDE)

    def at(a, b):
        xx = lax.rem(x + core * a + (1 - core) * b + 2 * SIDE, SIDE)
        yy = lax.rem(y + (1 - core) * a + core * b + 2 * SIDE, SIDE)
        return (xx * SIDE + yy) * 2 + core

    other = me + 1 - 2 * core
    peers = [at(1, 0), at(-1, 0), at(0, 1), at(0, -1), other]
    barrier = pltpu.get_barrier_semaphore()
    for peer in peers:
        pl.semaphore_signal(barrier, inc=1, device_id=along_gx(peer), device_id_type=MESH)
    pl.semaphore_wait(barrier, len(peers))

    def block(a, b, part=None):
        start = at(a, b) * rows
        if part is None:
            return whole.at[pl.ds(pl.multiple_of(start, rows), rows), :]
        return whole.at[pl.ds(pl.multiple_of(start + part * half, half), half), :]

    sent = []

    def send(a, b, part, peer, sem):
        source = own_ref if (a, b) == (0, 0) else block(a, b, part)
        copy = pltpu.make_async_remote_copy(
            src_ref=source,
            dst_ref=block(a, b, part),
            send_sem=send_sem.at[len(sent)],
            recv_sem=sem,
            device_id=along_gx(peer),
            device_id_type=MESH,
        )
        copy.start()
        sent.append(copy)

    crossed = []

    def cross(a, b):
        source = own_ref if (a, b) == (0, 0) else block(a, b)
        i = len(crossed)
        copy = pltpu.make_async_remote_copy(
            src_ref=source,
            dst_ref=block(a, b),
            send_sem=core_send.at[i],
            recv_sem=core_sem.at[i],
            device_id=along_gx(other),
            device_id_type=MESH,
        )
        copy.start()
        crossed.append(copy)

    def arrived(a, b, part, sem):
        ref = block(a, b, part)
        pltpu.make_async_copy(ref, ref, sem).wait()

    def spread(a):
        send(a, 0, None, peers[2], far_sem.at[a % SIDE, 0])
        send(a, 0, None, peers[3], far_sem.at[a % SIDE, 1])

    def spread_on(a):
        arrived(a, -1, None, far_sem.at[a % SIDE, 0])
        send(a, -1, 0, peers[2], far_sem.at[a % SIDE, 2])
        arrived(a, 1, None, far_sem.at[a % SIDE, 1])
        send(a, 1, 1, peers[3], far_sem.at[a % SIDE, 3])
        cross(a, -1)
        cross(a, 1)

    def spread_end(a):
        arrived(a, 2, 0, far_sem.at[a % SIDE, 2])
        arrived(a, 2, 1, far_sem.at[a % SIDE, 3])
        cross(a, 2)

    send(0, 0, None, peers[0], near_sem.at[0])
    send(0, 0, None, peers[1], near_sem.at[1])
    spread(0)
    cross(0, 0)
    mine = pltpu.make_async_copy(own_ref, block(0, 0), local_sem)
    mine.start()
    arrived(-1, 0, None, near_sem.at[0])
    send(-1, 0, 0, peers[0], near_sem.at[2])
    spread(-1)
    arrived(1, 0, None, near_sem.at[1])
    send(1, 0, 1, peers[1], near_sem.at[3])
    spread(1)
    cross(-1, 0)
    cross(1, 0)
    spread_on(0)
    arrived(2, 0, 0, near_sem.at[2])
    arrived(2, 0, 1, near_sem.at[3])
    spread(2)
    cross(2, 0)
    spread_on(-1)
    spread_end(0)
    spread_on(1)
    spread_end(-1)
    spread_on(2)
    spread_end(1)
    spread_end(2)
    mine.wait()
    for copy in sent:
        copy.wait_send()
    for copy in crossed:
        copy.wait()


def gather(own):
    rows, columns = own.shape
    return pl.pallas_call(
        gather_kernel,
        out_shape=jax.ShapeDtypeStruct((32 * rows, columns), own.dtype),
        in_specs=[pl.BlockSpec(memory_space=VMEM)],
        out_specs=pl.BlockSpec(memory_space=pl.ANY),
        scratch_shapes=[
            pltpu.SemaphoreType.DMA,
            pltpu.SemaphoreType.DMA((20,)),
            pltpu.SemaphoreType.DMA((4,)),
            pltpu.SemaphoreType.DMA((4, 4)),
            pltpu.SemaphoreType.DMA((16,)),
            pltpu.SemaphoreType.DMA((16,)),
        ],
        compiler_params=pltpu.CompilerParams(collective_id=0, has_side_effects=True),
        name="gather",
    )(own)


def dot(a, b, contract=(1, 0)):
    dims = (((contract[0],), (contract[1],)), ((), ()))
    return lax.dot_general(a, b, dims, precision=HIGH, preferred_element_type=jnp.float32)


def invert_block(load, ones, between):
    sub = lax.broadcasted_iota(jnp.int32, (W, B), 0)
    lane = lax.broadcasted_iota(jnp.int32, (W, B), 1)
    zero = jnp.zeros((W, B), jnp.float32)
    a = [load(i) for i in range(TILES)]
    low, scaled = [], []

    def row(t, j):
        return jnp.broadcast_to(t[j : j + 1, :], (W, B))

    def column(t, j):
        return jnp.broadcast_to(t[:, j : j + 1], (W, B))

    for g in range(0, TILES, GROUP):
        pair = range(g, g + GROUP)
        for i in pair:
            low.append(jnp.where(lane < g * W, a[i], jnp.where(lane == i * W + sub, 1.0, 0.0)))
        for p in pair:
            t = a[p]
            own = (lane >= p * W) & (lane < (p + 1) * W)
            others = [i for i in pair if i != p]
            b = [column(t, p * W + j) * ones for j in range(W)]
            c = {(i, j): column(a[i], p * W + j) for i in others for j in range(W)}
            t = jnp.where(own, jnp.where(lane == p * W + sub, 1.0, 0.0), t)
            for j in range(0, W, 2):
                k = j + 1
                first, both, second = row(b[j], j), row(b[k], j), row(b[k], k)
                f = 1.0 / (first * second - both * both)
                two = (sub == j) | (sub == k)
                m, n = jnp.where(two, 0.0, b[j]), jnp.where(two, 0.0, b[k])

                def eliminate(v):
                    vj, vk = row(v, j), row(v, k)
                    nj = (second * vj - both * vk) * f
                    nk = (first * vk - both * vj) * f
                    return jnp.where(sub == j, nj, jnp.where(sub == k, nk, v - (m * nj + n * nk)))

                b = [eliminate(b[q]) if q > k else None for q in range(W)]
                t = eliminate(t)
            rows = [row(t, j) for j in range(W)]
            for i in others:
                s = [c[i, 2 * h] * rows[2 * h] + c[i, 2 * h + 1] * rows[2 * h + 1] for h in range(W // 2)]
                a[i] = jnp.where(own, 0.0, a[i]) - ((s[0] + s[1]) + (s[2] + s[3]))
            a[p] = t
        end = (g + GROUP) * W
        scaled += [jnp.where(lane < end, a[i], 0.0) for i in pair]
        if g + GROUP < TILES:
            inside = (lane >= g * W) & (lane < end)
            weights = [zero] * g + [a[i] for i in pair] + [zero] * (TILES - g - GROUP)
            change = dot(jnp.concatenate(a[g + GROUP :], 0), jnp.concatenate(weights, 0))
            for n, i in enumerate(range(g + GROUP, TILES)):
                a[i] = jnp.where(inside, 0.0, a[i]) - change[n * W : (n + 1) * W]
        between(g // GROUP)
    return dot(jnp.concatenate(low, 0), jnp.concatenate(scaled, 0), (0, 0))


def inverse_kernel(e_ref, t_ref, e, panels, unit, scale):
    own, size = t_ref.shape
    blocks = size // B
    first = lax.axis_index("gx") * own
    at = lax.broadcasted_iota(jnp.int32, (own, size), 1) - lax.broadcasted_iota(jnp.int32, (own, size), 0)
    eye = lax.broadcasted_iota(jnp.int32, (B, B), 0) == lax.broadcasted_iota(jnp.int32, (B, B), 1)
    waiting = []

    def between(i):
        left = TILES // GROUP - 1 - i
        count = len(waiting) if left == 0 else -(-len(waiting) // (left + 1))
        for _ in range(count):
            waiting.pop(0)()

    def span(k):
        return slice(k * B, (k + 1) * B)

    by_row = []
    for k in range(blocks):
        diagonal = jnp.where(eye, e_ref[span(k), span(k)], 0.0)
        scale[:, span(k)] = lax.rsqrt(jnp.sum(diagonal, axis=0, keepdims=True))
        by_row.append(lax.rsqrt(jnp.sum(diagonal, axis=1, keepdims=True)))
    for k in range(blocks):
        upper = slice(k * B, size)
        e[span(k), upper] = e_ref[span(k), upper] * by_row[k] * scale[:, upper]
    unit[...] = jnp.where(at == first, scale[...], 0.0)
    ones = jnp.broadcast_to(jnp.minimum(scale[:, :B] + 1.0, 1.0), (W, B))

    def trail(k, i, columns):
        e[span(i), columns] -= dot(e[span(k), span(i)], panels[span(k), columns], (0, 0))

    for k in range(blocks):
        d = invert_block(lambda i: e[k * B + i * W : k * B + (i + 1) * W, span(k)], ones, between)
        if k + 1 < blocks:
            after = slice((k + 1) * B, size)
            panels[span(k), span(k + 1)] = dot(d, e[span(k), span(k + 1)])
            trail(k, k + 1, span(k + 1))

            def rest(k=k, d=d):
                far = slice((k + 2) * B, size)
                panels[span(k), far] = dot(d, e[span(k), far])

            def across(k=k, after=after):
                unit[:, after] -= dot(unit[:, span(k)], panels[span(k), after])

            if k + 2 < blocks:
                waiting.append(rest)
                for i in range(k + 1, blocks):
                    for j in range(max(i, k + 2), blocks, 2):
                        columns = slice(j * B, min(j + 2, blocks) * B)
                        waiting.append(lambda k=k, i=i, columns=columns: trail(k, i, columns))
            waiting.append(across)
        waiting.append(lambda k=k, d=d: t_ref.__setitem__((slice(None), span(k)), dot(unit[:, span(k)], d)))
    for work in waiting:
        work()
    for k in reversed(range(blocks - 1)):
        after = slice((k + 1) * B, size)
        t_ref[:, span(k)] -= dot(t_ref[:, after], panels[span(k), after], (1, 1))
    t_ref[...] *= scale[...]


def inverse_rows(whole, own):
    size = whole.shape[0]
    return pl.pallas_call(
        inverse_kernel,
        out_shape=jax.ShapeDtypeStruct((own, size), jnp.float32),
        in_specs=[pl.BlockSpec(memory_space=VMEM)],
        out_specs=pl.BlockSpec(memory_space=VMEM),
        scratch_shapes=[
            VMEM((size, size), jnp.float32),
            VMEM((size, size), jnp.float32),
            VMEM((own, size), jnp.float32),
            VMEM((1, size), jnp.float32),
        ],
        compiler_params=pltpu.CompilerParams(vmem_limit_bytes=48 * 2**20),
        name="inverse_rows",
    )(whole)


def total(a):
    return jnp.sum(jnp.sum(a, axis=0, keepdims=True), axis=1, keepdims=True)


def cg_kernel(
    n_gx, n_gy, rhs_ref, shift_ref, fx_ref, fy_ref, mask_ref, v_ref, t_ref, x_ref, res_ref,
    u0_ref, w0_ref, z1_ref, s1_ref, cu_ref, cl_ref, diag_ref, y_ref,
    msg, coef, sums, group, line, edge_out, edge_in, face_out, face_in,
    coef_send, coef_recv, group_send, group_recv, line_send, line_recv, edge_send, edge_recv, face_send, face_recv,
):
    vectors, cx_n, cy_n = v_ref.shape
    gx, gy = lax.axis_index("gx"), lax.axis_index("gy")
    lane1 = lax.broadcasted_iota(jnp.int32, (1, cy_n), 1)
    row2 = lax.broadcasted_iota(jnp.int32, (cx_n, cy_n), 0)
    lane2 = lax.broadcasted_iota(jnp.int32, (cx_n, cy_n), 1)
    eye = row2 == lane2

    def along(axis, count, step):
        return {axis: lax.rem(lax.axis_index(axis) + step, count)}

    below, above = along("gx", n_gx, 1), along("gx", n_gx, n_gx - 1)
    right, left = along("gy", n_gy, 1), along("gy", n_gy, n_gy - 1)

    barrier = pltpu.get_barrier_semaphore()
    for axis, count in (("gx", n_gx), ("gy", n_gy)):

        def greet(step, carry, axis=axis, count=count):
            pl.semaphore_signal(barrier, inc=1, device_id=along(axis, count, step), device_id_type=MESH)
            return carry

        lax.fori_loop(1, count, greet, 0)

    mask = mask_ref[...].astype(jnp.float32)
    cx = fx_ref[...] * mask
    cy = fy_ref[...] * mask
    self_term = shift_ref[...] * mask + (1.0 - mask)

    def as_row(column):
        return jnp.sum(jnp.where(eye, column, 0.0), axis=0, keepdims=True)

    def as_column(row):
        return jnp.sum(jnp.where(eye, row, 0.0), axis=1, keepdims=True)

    face_out[0] = cx[cx_n - 1 :, :]
    face_out[1] = as_row(cy[:, cy_n - 1 :])

    def coefficients(field):
        parts = jnp.sum(v_ref[...] * field[None], axis=1)
        column = jnp.sum(parts, axis=1, keepdims=True)
        place = lax.rem(gx, cy_n // vectors) * vectors + lax.broadcasted_iota(jnp.int32, (vectors, cy_n), 0)
        here = lax.broadcasted_iota(jnp.int32, (vectors, cy_n), 1) == place
        return jnp.sum(jnp.where(here, column, 0.0), axis=0, keepdims=True)

    first = coefficients(rhs_ref[...])

    pl.semaphore_wait(barrier, n_gx + n_gy - 2)

    faces = []
    for i, (peer, name) in enumerate(((below, "x"), (right, "y"))):
        copy = pltpu.make_async_remote_copy(
            src_ref=face_out.at[i], dst_ref=face_in.at[i], send_sem=face_send.at[i], recv_sem=face_recv.at[i],
            device_id=peer, device_id_type=MESH,
        )
        copy.start()
        faces.append(copy)

    def share(source, slots, axis, count, send, recv):
        me = lax.axis_index(axis)
        slots[me] = source[...]

        def one(step, carry):
            pltpu.make_async_remote_copy(
                src_ref=source, dst_ref=slots.at[me], send_sem=send, recv_sem=recv,
                device_id=along(axis, count, step), device_id_type=MESH,
            ).start()
            return carry

        lax.fori_loop(1, count, one, 0)

    def shared(slots, count, send, recv):
        others = slots.at[pl.ds(0, count - 1)]
        pltpu.make_async_copy(others, others, recv).wait()
        pltpu.make_async_copy(others, others, send).wait()

    def send_coefficients(i, row):
        msg[i] = row
        share(msg.at[i], coef.at[i], "gx", n_gx, coef_send.at[i], coef_recv.at[i])

    def gathered(i):
        shared(coef.at[i], n_gx, coef_send.at[i], coef_recv.at[i])
        each = cy_n // vectors
        return [sum(coef[i, p * each + j] for j in range(1, each)) + coef[i, p * each] for p in range(n_gx // each)]

    def expand(rows):
        acc = sum(t_ref[:, p * cy_n : (p + 1) * cy_n] * row for p, row in enumerate(rows))
        y_ref[...] = jnp.broadcast_to(jnp.sum(acc, axis=1, keepdims=True), (vectors, cy_n))
        out = v_ref[0] * y_ref[0:1, :]
        for k in range(1, vectors):
            out = out + v_ref[k] * y_ref[k : k + 1, :]
        return out

    def apply(i, field):
        edge_out[i, 0] = field[cx_n - 1 :, :]
        edge_out[i, 1] = field[0:1, :]
        edge_out[i, 2] = as_row(field[:, cy_n - 1 :])
        edge_out[i, 3] = as_row(field[:, 0:1])
        copies = []
        for j, peer in enumerate((below, above, right, left)):
            copy = pltpu.make_async_remote_copy(
                src_ref=edge_out.at[i, j], dst_ref=edge_in.at[i, j],
                send_sem=edge_send.at[i, j], recv_sem=edge_recv.at[i, j],
                device_id=peer, device_id_type=MESH,
            )
            copy.start()
            copies.append(copy)
        down = pltpu.roll(field, cx_n - 1, 0)
        up = pltpu.roll(field, 1, 0)
        to_right = pltpu.roll(field, cy_n - 1, 1)
        to_left = pltpu.roll(field, 1, 1)
        for copy in copies:
            copy.wait()
        zero = jnp.zeros((1, cy_n), jnp.float32)
        from_above = jnp.where(gx > 0, edge_in[i, 0], zero)
        from_below = jnp.where(gx < n_gx - 1, edge_in[i, 1], zero)
        from_left = jnp.where(gy > 0, edge_in[i, 2], zero)
        from_right = jnp.where(gy < n_gy - 1, edge_in[i, 3], zero)
        down = jnp.where(row2 == cx_n - 1, from_below, down)
        up = jnp.where(row2 == 0, from_above, up)
        to_right = jnp.where(lane2 == cy_n - 1, as_column(from_right), to_right)
        to_left = jnp.where(lane2 == 0, as_column(from_left), to_left)
        mask = mask_ref[...].astype(jnp.float32)
        self_term = shift_ref[...] * mask + (1.0 - mask)
        return (
            self_term * field
            + fx_ref[...] * mask * (field - down)
            + cu_ref[...] * (field - up)
            + fy_ref[...] * mask * (field - to_right)
            + cl_ref[...] * (field - to_left)
        )

    def packed(values):
        row = jnp.zeros((1, cy_n), jnp.float32)
        for i, value in enumerate(values):
            row = jnp.where(lane1 == i, value, row)
        return row

    def sum_over_group(i, values):
        sums[i, 0] = packed(values)
        share(sums.at[i, 0], group.at[i], "gx", n_gx, group_send.at[i], group_recv.at[i])

    def sum_over_lines(i):
        shared(group.at[i], n_gx, group_send.at[i], group_recv.at[i])
        sums[i, 1] = sum(group[i, d] for d in range(1, n_gx)) + group[i, 0]
        share(sums.at[i, 1], line.at[i], "gy", n_gy, line_send.at[i], line_recv.at[i])

    def summed(i):
        shared(line.at[i], n_gy, line_send.at[i], line_recv.at[i])
        row = sum(line[i, d] for d in range(1, n_gy)) + line[i, 0]

        def value(j):
            return jnp.sum(jnp.where(lane1 == j, row, 0.0), axis=1, keepdims=True)

        return value

    send_coefficients(0, first)
    for copy in faces:
        copy.wait()
    upper = jnp.where(gx > 0, face_in[0], jnp.zeros((1, cy_n), jnp.float32))
    beside = jnp.where(gy > 0, face_in[1], jnp.zeros((1, cy_n), jnp.float32))
    cu = jnp.where(row2 == 0, upper, pltpu.roll(cx, 1, 0))
    cl = jnp.where(lane2 == 0, as_column(beside), pltpu.roll(cy, 1, 1))
    cu_ref[...] = cu
    cl_ref[...] = cl
    inverse_diag = 1.0 / (self_term + cx + cu + cy + cl)
    diag_ref[...] = inverse_diag
    u0 = rhs_ref[...] * inverse_diag + expand(gathered(0))
    u0_ref[...] = u0
    w0 = apply(0, u0)
    w0_ref[...] = w0

    send_coefficients(1, coefficients(w0))
    sum_over_group(0, [total(rhs_ref[...] * u0), total(u0 * w0)])
    rows_w0 = gathered(1)
    u1 = w0_ref[...] * diag_ref[...] + expand(rows_w0)
    sum_over_lines(0)
    w1 = apply(1, u1)

    send_coefficients(2, coefficients(w1))
    rows_w1 = gathered(2)
    value = summed(0)
    g00 = value(1)
    alpha0 = value(0) / g00
    z1 = u0_ref[...] - alpha0 * u1
    s1 = w0_ref[...] - alpha0 * w1
    z1_ref[...] = z1
    s1_ref[...] = s1
    q = alpha0 * s1 * diag_ref[...] + expand([alpha0 * (a - alpha0 * b) for a, b in zip(rows_w0, rows_w1)])
    v = apply(2, q)

    r1 = rhs_ref[...] - alpha0 * w0_ref[...]
    u0, z1, s1 = u0_ref[...], z1_ref[...], s1_ref[...]
    sum_over_group(1, [total(u0 * s1), total(u0 * v), total(z1 * s1), total(z1 * v), total(q * v), total(z1 * r1), total(q * r1)])
    sum_over_lines(1)
    value = summed(1)
    g01, g02, g11, g12, g22, b1, b2 = [value(j) for j in range(7)]
    l10 = g01 / g00
    l20 = g02 / g00
    d1 = g11 - l10 * g01
    e12 = g12 - l20 * g01
    l21 = e12 / d1
    d2 = g22 - l20 * g02 - l21 * e12
    c2 = (b2 - l21 * b1) / d2
    c1 = b1 / d1 - l21 * c2
    c0 = -(l10 * c1 + l20 * c2)
    x_ref[...] = (alpha0 + c0) * u0 + c1 * z1 + c2 * q
    res_ref[...] = r1 - c0 * w0_ref[...] - c1 * s1 - c2 * v


def conjugate_gradients(n_gx, n_gy, *args):
    tile = args[0].shape
    vectors, _, lanes = args[5].shape
    field = VMEM(tile, jnp.float32)
    dma = pltpu.SemaphoreType.DMA
    f32 = jnp.float32
    return pl.pallas_call(
        functools.partial(cg_kernel, n_gx, n_gy),
        out_shape=(jax.ShapeDtypeStruct(tile, f32),) * 2,
        in_specs=[pl.BlockSpec(memory_space=VMEM)] * 7,
        out_specs=(pl.BlockSpec(memory_space=VMEM),) * 2,
        scratch_shapes=[field] * 7
        + [
            VMEM((vectors, lanes), f32),
            VMEM((3, 1, lanes), f32),
            VMEM((3, n_gx, 1, lanes), f32),
            VMEM((2, 2, 1, lanes), f32),
            VMEM((2, n_gx, 1, lanes), f32),
            VMEM((2, n_gy, 1, lanes), f32),
            VMEM((3, 4, 1, lanes), f32),
            VMEM((3, 4, 1, lanes), f32),
            VMEM((2, 1, lanes), f32),
            VMEM((2, 1, lanes), f32),
            dma((3,)), dma((3,)), dma((2,)), dma((2,)), dma((2,)), dma((2,)),
            dma((3, 4)), dma((3, 4)), dma((2,)), dma((2,)),
        ],
        compiler_params=pltpu.CompilerParams(collective_id=1, has_side_effects=True, vmem_limit_bytes=32 * 2**20),
        name="conjugate_gradients",
    )(*args)


def body(n_gx, n_gy, right_side, shift, face_x, face_y, ice_mask, deflation, coarse_matrix):
    whole = gather(coarse_matrix[0])
    rows = inverse_rows(whole, coarse_matrix.shape[1])
    return conjugate_gradients(n_gx, n_gy, right_side, shift, face_x, face_y, ice_mask, deflation, rows)


def solution(mesh):
    in_specs = (
        P("gx", "gy"),
        P("gx", "gy"),
        P("gx", "gy"),
        P("gx", "gy"),
        P("gx", "gy"),
        P(None, "gx", "gy"),
        P("gy", "gx", None),
    )
    out_specs = (P("gx", "gy"), P("gx", "gy"))
    run = functools.partial(body, mesh.shape["gx"], mesh.shape["gy"])
    return jax.shard_map(run, mesh=mesh, in_specs=in_specs, out_specs=out_specs, check_vma=False)
```

profile of v0, /device:TPU:1, one launch (start us, length us, event | category | flops | bytes accessed | tf_op | source)
XLA Modules:
  0.0 120.8 jit_solution(13473947186979052417)
XLA Ops:
  0.6 0.0 copy-start.1
  0.6 0.0 copy-start.2
  0.7 0.0 copy-start.3
  0.7 0.0 copy-start.4
  0.7 0.0 copy-start.5
  0.7 0.0 copy-start.6
  0.7 31.4 %gather.1.e_ref = f32[1024,1024]{1,0:T(8,128)} custom-call(f32[32,1024]{1,0:T(8,128)} %bitcast.1), custom_call_target="tpu_custom_call" | custom-call | tf_op jit(solution)/shard_map/gather/pallas_call | solution.py:137
  32.1 0.0 copy-start
  32.1 2.2 %copy-done = f32[1024,1024]{1,0:T(8,128)S(1)} copy-done((f32[1024,1024]{1,0:T(8,128)S(1)}, f32[1024,1024]{1,0:T(8,128)}, u32[]{:S(2)}) %copy-start) | copy-done | bytes 4194328
  34.3 36.6 %inverse_rows.1.t_ref = f32[32,1024]{1,0:T(8,128)S(1)} custom-call(f32[1024,1024]{1,0:T(8,128)S(1)} %copy-done), custom_call_target="tpu_custom_call" | custom-call | tf_op jit(solution)/shard_map/inverse_rows/pallas_call | solution.py:279
  70.8 0.0 copy-done.1
  70.9 0.0 copy-done.2
  70.9 0.0 copy-done.3
  70.9 0.0 copy-done.4
  70.9 0.0 copy-done.5
  70.9 0.0 copy-done.6
  70.9 48.6 %conjugate_gradients.1 = (f32[128,128]{1,0:T(8,128)S(1)}, f32[128,128]{1,0:T(8,128)S(1)}) custom-call(f32[128,128]{1,0:T(8,128)S(1)} %copy-done.2, f32[128,128]{1,0:T(8,128)S(1)} %copy-done.3, f32[128,128]{1,0:T(8,128)S(1)} %copy-done.4, f32[128,128]{1,0:T(8,128)S(1)} %copy-done.5, s32[128,128]{1,0:T(8,128)S(1)} %copy-done.6, f32[32,128,128]{2,1,0:T(8,128)S(1)} %copy-done.1, ...), custom_call_target="tpu_custom_call" | custom-call | tf_op jit(solution)/shard_map/conjugate_gradients/pallas_call | solution.py:519
  119.6 0.6 copy.11
  120.2 0.6 copy.12
Async XLA Ops:
  0.6 70.2 %copy-start.1 = (f32[32,128,128]{2,1,0:T(8,128)S(1)}, f32[32,128,128]{2,1,0:T(8,128)}, u32[]{:S(2)}) copy-start(f32[32,128,128]{2,1,0:T(8,128)} %v_ref.1) | copy-start | bytes 6291460
  0.6 70.2 %copy-start.2 = (f32[128,128]{1,0:T(8,128)S(1)}, f32[128,128]{1,0:T(8,128)}, u32[]{:S(2)}) copy-start(f32[128,128]{1,0:T(8,128)} %rhs_ref.1) | copy-start | bytes 196612
  0.7 70.2 %copy-start.3 = (f32[128,128]{1,0:T(8,128)S(1)}, f32[128,128]{1,0:T(8,128)}, u32[]{:S(2)}) copy-start(f32[128,128]{1,0:T(8,128)} %shift_ref.1) | copy-start | bytes 196612
  0.7 70.2 %copy-start.4 = (f32[128,128]{1,0:T(8,128)S(1)}, f32[128,128]{1,0:T(8,128)}, u32[]{:S(2)}) copy-start(f32[128,128]{1,0:T(8,128)} %fx_ref.1) | copy-start | bytes 196612
  0.7 70.2 %copy-start.5 = (f32[128,128]{1,0:T(8,128)S(1)}, f32[128,128]{1,0:T(8,128)}, u32[]{:S(2)}) copy-start(f32[128,128]{1,0:T(8,128)} %fy_ref.1) | copy-start | bytes 196612
  0.7 70.2 %copy-start.6 = (s32[128,128]{1,0:T(8,128)S(1)}, s32[128,128]{1,0:T(8,128)}, u32[]{:S(2)}) copy-start(s32[128,128]{1,0:T(8,128)} %mask_ref.1) | copy-start | bytes 196612
  32.1 2.2 %copy-start = (f32[1024,1024]{1,0:T(8,128)S(1)}, f32[1024,1024]{1,0:T(8,128)}, u32[]{:S(2)}) copy-start(f32[1024,1024]{1,0:T(8,128)} %gather.1.e_ref) | copy-start | bytes 12582916
where the time goes:
time: 121 us
  Pallas kernels  117 us (97%)
  local copies, waits for them, and re-layouts  3.47 us (3%)
    pallas_call x1, Pallas kernels, conjugate_gradients(): pl.pallas_call(functools.partial(cg_kernel, n_gx, n_gy), out_shape=(jax.S...  48.6 us
    pallas_call x1, Pallas kernels, inverse_rows(): pl.pallas_call(inverse_kernel, out_shape=jax.ShapeDtypeStruct((own, size)...  36.6 us
    pallas_call x1, Pallas kernels, gather(): pl.pallas_call(gather_kernel, out_shape=jax.ShapeDtypeStruct((32 * rows,...  31.4 us
    unnamed x16, local copies, waits for them, and re-layouts  3.47 us

commit v1 on v0

--- a/solution.py
+++ b/solution.py
@@ -362,14 +362,11 @@
         me = lax.axis_index(axis)
         slots[me] = source[...]
 
-        def one(step, carry):
+        for step in sorted(range(1, count), key=lambda s: abs(s - count // 2)):
             pltpu.make_async_remote_copy(
                 src_ref=source, dst_ref=slots.at[me], send_sem=send, recv_sem=recv,
                 device_id=along(axis, count, step), device_id_type=MESH,
             ).start()
-            return carry
-
-        lax.fori_loop(1, count, one, 0)
 
     def shared(slots, count, send, recv):
         others = slots.at[pl.ds(0, count - 1)]

time: 121 us -> 120 us (level)
  no operation moved by 1% of the time
where the time goes in v1:
time: 120 us
  Pallas kernels  116 us (97%)
  local copies, waits for them, and re-layouts  3.47 us (3%)
    pallas_call x1, Pallas kernels, conjugate_gradients(): pl.pallas_call(functools.partial(cg_kernel, n_gx, n_gy), out_shape=(jax.S...  47.8 us
    pallas_call x1, Pallas kernels, inverse_rows(): pl.pallas_call(inverse_kernel, out_shape=jax.ShapeDtypeStruct((own, size)...  36.6 us
    pallas_call x1, Pallas kernels, gather(): pl.pallas_call(gather_kernel, out_shape=jax.ShapeDtypeStruct((32 * rows,...  31.4 us
    unnamed x16, local copies, waits for them, and re-layouts  3.47 us

profile of v1, /device:TPU:1, one launch (start us, length us, event | category | flops | bytes accessed | tf_op | source)
XLA Modules:
  0.0 120.0 jit_solution(8763697202476868651)
XLA Ops:
  0.6 0.0 copy-start.1
  0.6 0.0 copy-start.2
  0.7 0.0 copy-start.3
  0.7 0.0 copy-start.4
  0.7 0.0 copy-start.5
  0.7 0.0 copy-start.6
  0.7 31.4 %gather.1.e_ref = f32[1024,1024]{1,0:T(8,128)} custom-call(f32[32,1024]{1,0:T(8,128)} %bitcast.1), custom_call_target="tpu_custom_call" | custom-call | tf_op jit(solution)/shard_map/gather/pallas_call | solution.py:137
  32.1 0.0 copy-start
  32.1 2.2 %copy-done = f32[1024,1024]{1,0:T(8,128)S(1)} copy-done((f32[1024,1024]{1,0:T(8,128)S(1)}, f32[1024,1024]{1,0:T(8,128)}, u32[]{:S(2)}) %copy-start) | copy-done | bytes 4194328
  34.3 36.6 %inverse_rows.1.t_ref = f32[32,1024]{1,0:T(8,128)S(1)} custom-call(f32[1024,1024]{1,0:T(8,128)S(1)} %copy-done), custom_call_target="tpu_custom_call" | custom-call | tf_op jit(solution)/shard_map/inverse_rows/pallas_call | solution.py:279
  70.8 0.0 copy-done.1
  70.9 0.0 copy-done.2
  70.9 0.0 copy-done.3
  70.9 0.0 copy-done.4
  70.9 0.0 copy-done.5
  70.9 0.0 copy-done.6
  70.9 47.8 %conjugate_gradients.1 = (f32[128,128]{1,0:T(8,128)S(1)}, f32[128,128]{1,0:T(8,128)S(1)}) custom-call(f32[128,128]{1,0:T(8,128)S(1)} %copy-done.2, f32[128,128]{1,0:T(8,128)S(1)} %copy-done.3, f32[128,128]{1,0:T(8,128)S(1)} %copy-done.4, f32[128,128]{1,0:T(8,128)S(1)} %copy-done.5, s32[128,128]{1,0:T(8,128)S(1)} %copy-done.6, f32[32,128,128]{2,1,0:T(8,128)S(1)} %copy-done.1, ...), custom_call_target="tpu_custom_call" | custom-call | tf_op jit(solution)/shard_map/conjugate_gradients/pallas_call | solution.py:516
  118.7 0.6 copy.11
  119.3 0.6 copy.12
Async XLA Ops:
  0.6 70.2 %copy-start.1 = (f32[32,128,128]{2,1,0:T(8,128)S(1)}, f32[32,128,128]{2,1,0:T(8,128)}, u32[]{:S(2)}) copy-start(f32[32,128,128]{2,1,0:T(8,128)} %v_ref.1) | copy-start | bytes 6291460
  0.6 70.2 %copy-start.2 = (f32[128,128]{1,0:T(8,128)S(1)}, f32[128,128]{1,0:T(8,128)}, u32[]{:S(2)}) copy-start(f32[128,128]{1,0:T(8,128)} %rhs_ref.1) | copy-start | bytes 196612
  0.7 70.2 %copy-start.3 = (f32[128,128]{1,0:T(8,128)S(1)}, f32[128,128]{1,0:T(8,128)}, u32[]{:S(2)}) copy-start(f32[128,128]{1,0:T(8,128)} %shift_ref.1) | copy-start | bytes 196612
  0.7 70.2 %copy-start.4 = (f32[128,128]{1,0:T(8,128)S(1)}, f32[128,128]{1,0:T(8,128)}, u32[]{:S(2)}) copy-start(f32[128,128]{1,0:T(8,128)} %fx_ref.1) | copy-start | bytes 196612
  0.7 70.2 %copy-start.5 = (f32[128,128]{1,0:T(8,128)S(1)}, f32[128,128]{1,0:T(8,128)}, u32[]{:S(2)}) copy-start(f32[128,128]{1,0:T(8,128)} %fy_ref.1) | copy-start | bytes 196612
  0.7 70.2 %copy-start.6 = (s32[128,128]{1,0:T(8,128)S(1)}, s32[128,128]{1,0:T(8,128)}, u32[]{:S(2)}) copy-start(s32[128,128]{1,0:T(8,128)} %mask_ref.1) | copy-start | bytes 196612
  32.1 2.2 %copy-start = (f32[1024,1024]{1,0:T(8,128)S(1)}, f32[1024,1024]{1,0:T(8,128)}, u32[]{:S(2)}) copy-start(f32[1024,1024]{1,0:T(8,128)} %gather.1.e_ref) | copy-start | bytes 12582916

commit v2 on v1

--- a/solution.py
+++ b/solution.py
@@ -14,7 +14,7 @@
 B = 128
 W = 8
 TILES = B // W
-GROUP = 4
+GROUP = 2
 
 
 def along_gx(index):

time: 120 us -> 121 us (level)
    pallas_call x1, Pallas kernels: 36.6 us -> 37.8 us  [inverse_rows(): pl.pallas_call(inverse_kernel, out_shape=jax.ShapeDtypeStruct((own, size)...]
where the time goes in v2:
time: 121 us
  Pallas kernels  117 us (97%)
  local copies, waits for them, and re-layouts  3.47 us (3%)
    pallas_call x1, Pallas kernels, conjugate_gradients(): pl.pallas_call(functools.partial(cg_kernel, n_gx, n_gy), out_shape=(jax.S...  47.8 us
    pallas_call x1, Pallas kernels, inverse_rows(): pl.pallas_call(inverse_kernel, out_shape=jax.ShapeDtypeStruct((own, size)...  37.8 us
    pallas_call x1, Pallas kernels, gather(): pl.pallas_call(gather_kernel, out_shape=jax.ShapeDtypeStruct((32 * rows,...  31.4 us
    unnamed x16, local copies, waits for them, and re-layouts  3.47 us

profile of v2, /device:TPU:1, one launch (start us, length us, event | category | flops | bytes accessed | tf_op | source)
XLA Modules:
  0.0 121.2 jit_solution(6437795417414329054)
XLA Ops:
  0.6 0.0 copy-start.1
  0.6 0.0 copy-start.2
  0.7 0.0 copy-start.3
  0.7 0.0 copy-start.4
  0.7 0.0 copy-start.5
  0.7 0.0 copy-start.6
  0.7 31.4 %gather.1.e_ref = f32[1024,1024]{1,0:T(8,128)} custom-call(f32[32,1024]{1,0:T(8,128)} %bitcast.1), custom_call_target="tpu_custom_call" | custom-call | tf_op jit(solution)/shard_map/gather/pallas_call | solution.py:137
  32.1 0.0 copy-start
  32.1 2.2 %copy-done = f32[1024,1024]{1,0:T(8,128)S(1)} copy-done((f32[1024,1024]{1,0:T(8,128)S(1)}, f32[1024,1024]{1,0:T(8,128)}, u32[]{:S(2)}) %copy-start) | copy-done | bytes 4194328
  34.3 37.8 %inverse_rows.1.t_ref = f32[32,1024]{1,0:T(8,128)S(1)} custom-call(f32[1024,1024]{1,0:T(8,128)S(1)} %copy-done), custom_call_target="tpu_custom_call" | custom-call | tf_op jit(solution)/shard_map/inverse_rows/pallas_call | solution.py:279
  72.1 0.0 copy-done.1
  72.1 0.0 copy-done.2
  72.1 0.0 copy-done.3
  72.1 0.0 copy-done.4
  72.1 0.0 copy-done.5
  72.1 0.0 copy-done.6
  72.1 47.8 %conjugate_gradients.1 = (f32[128,128]{1,0:T(8,128)S(1)}, f32[128,128]{1,0:T(8,128)S(1)}) custom-call(f32[128,128]{1,0:T(8,128)S(1)} %copy-done.2, f32[128,128]{1,0:T(8,128)S(1)} %copy-done.3, f32[128,128]{1,0:T(8,128)S(1)} %copy-done.4, f32[128,128]{1,0:T(8,128)S(1)} %copy-done.5, s32[128,128]{1,0:T(8,128)S(1)} %copy-done.6, f32[32,128,128]{2,1,0:T(8,128)S(1)} %copy-done.1, ...), custom_call_target="tpu_custom_call" | custom-call | tf_op jit(solution)/shard_map/conjugate_gradients/pallas_call | solution.py:516
  119.9 0.6 copy.11
  120.5 0.6 copy.12
Async XLA Ops:
  0.6 71.4 %copy-start.1 = (f32[32,128,128]{2,1,0:T(8,128)S(1)}, f32[32,128,128]{2,1,0:T(8,128)}, u32[]{:S(2)}) copy-start(f32[32,128,128]{2,1,0:T(8,128)} %v_ref.1) | copy-start | bytes 6291460
  0.6 71.5 %copy-start.2 = (f32[128,128]{1,0:T(8,128)S(1)}, f32[128,128]{1,0:T(8,128)}, u32[]{:S(2)}) copy-start(f32[128,128]{1,0:T(8,128)} %rhs_ref.1) | copy-start | bytes 196612
  0.7 71.5 %copy-start.3 = (f32[128,128]{1,0:T(8,128)S(1)}, f32[128,128]{1,0:T(8,128)}, u32[]{:S(2)}) copy-start(f32[128,128]{1,0:T(8,128)} %shift_ref.1) | copy-start | bytes 196612
  0.7 71.5 %copy-start.4 = (f32[128,128]{1,0:T(8,128)S(1)}, f32[128,128]{1,0:T(8,128)}, u32[]{:S(2)}) copy-start(f32[128,128]{1,0:T(8,128)} %fx_ref.1) | copy-start | bytes 196612
  0.7 71.5 %copy-start.5 = (f32[128,128]{1,0:T(8,128)S(1)}, f32[128,128]{1,0:T(8,128)}, u32[]{:S(2)}) copy-start(f32[128,128]{1,0:T(8,128)} %fy_ref.1) | copy-start | bytes 196612
  0.7 71.5 %copy-start.6 = (s32[128,128]{1,0:T(8,128)S(1)}, s32[128,128]{1,0:T(8,128)}, u32[]{:S(2)}) copy-start(s32[128,128]{1,0:T(8,128)} %mask_ref.1) | copy-start | bytes 196612
  32.1 2.2 %copy-start = (f32[1024,1024]{1,0:T(8,128)S(1)}, f32[1024,1024]{1,0:T(8,128)}, u32[]{:S(2)}) copy-start(f32[1024,1024]{1,0:T(8,128)} %gather.1.e_ref) | copy-start | bytes 12582916
